TPU v7x, 512 devices: a whole 4x8x8 slice. The times are simulated.
512 devices in a mesh: gs: 128 (over y, z, core), view: 4 (over x).
Axes of the slice: x: 4, y: 8, z: 8, core: 2. Of those that a mesh axis runs over, the one named last changes fastest.
Arguments:
- features: bfloat16 [131072, 128], P('gs'), may hold values from -6 to 6
- geometry: float32 [4, 9, 131072], P('view', None, 'gs'), as said below
- decoder: bfloat16 [128, 512], replicated, may hold values from -0.5 to 0.5
- teacher: bfloat16 [4, 131072, 512], P('view', 'gs'), may hold values from -3 to 3
- images: float32 [4, 3, 131072], P('view', None, 'gs'), may hold values from 0 to 1
- send_index: int32 [4, 128, 1024], P('view', 'gs'), may hold values from 0 to 1023, as said below
- tile_lists: int32 [4, 512, 8], P('view', 'gs'), may hold values from 0 to 7, as said below
- tile_lengths: int32 [4, 512], P('view', 'gs'), may hold values from 2 to 8
Outputs:
- feature_grad: float32 [131072, 128], P(('gs', 'view'))
- geometry_grad: float32 [4, 9, 131072], P('view', None, 'gs')
- decoder_grad: float32 [128, 512], replicated
Inputs may be any that keep to these rules, and one draw needn't show every extreme that they name: `send_index`: each row (one view, one source device) is a permutation of 0 .. 1023; positions k * 8 to (k + 1) * 8 - 1 hold the Gaussians sent to the device of gs index k. `tile_lists`: the 8 entries of a row are distinct. `geometry`: opacity logits lie in -7.5 .. -4, log conics between -2 log 16 and -2 log 16 + 2 log 4, shears in -2 .. 2, colors in 0 .. 1.
All inputs are finite; a program needn't handle non-finite values.
Results may differ from a plain program's by a relative error of at most 0.0017.
Values may be sent and summed in bfloat16 or wider, within the bound.
A program may use at most 64 MiB of HBM per device.

v0:
```python
import math
import jax
import jax.numpy as jnp
from jax import lax
from jax.sharding import PartitionSpec as P

FEAT = 128
CT = 512
TS = 16
BLK = 128
LIST = 8


def composite(tile_geo, alive_mask, pixel_x, pixel_y):
    delta_x = pixel_x[:, None] - tile_geo[0][None, :]
    delta_y = pixel_y[:, None] - tile_geo[1][None, :]
    conic_a = jnp.exp(tile_geo[2])
    conic_c = jnp.exp(tile_geo[3])
    conic_b = 0.8 * jnp.tanh(tile_geo[4]) * jnp.exp(0.5 * (tile_geo[2] + tile_geo[3]))
    exponent = -0.5 * (
        conic_a * delta_x * delta_x
        + 2.0 * conic_b * delta_x * delta_y
        + conic_c * delta_y * delta_y
    )
    opacity = alive_mask * jax.nn.sigmoid(tile_geo[5])
    alpha_val = opacity[None, :] * jnp.exp(exponent)
    log_keep = jnp.log1p(-alpha_val)
    pixel_count = pixel_x.shape[0]
    blocked = log_keep.reshape(pixel_count, LIST, BLK)
    inner = jnp.cumsum(blocked, axis=2) - blocked
    block_sums = jnp.sum(blocked, axis=2)
    outer = jnp.cumsum(block_sums, axis=1) - block_sums
    before = (inner + outer[:, :, None]).reshape(pixel_count, LIST * BLK)
    weights = alpha_val * jnp.exp(before)
    pixel_color = jnp.einsum("pi,ci->cp", weights, tile_geo[6:9], precision=lax.Precision.HIGHEST)
    return (weights, pixel_color)


def device_terms(
    recv_geo, recv_feat, decoder, teacher_dev, images_dev, lists, lengths, shard_index
):
    nblocks = recv_feat.shape[0] // BLK
    tile_pixels = TS * TS
    geo_blocks = recv_geo.reshape(9, nblocks, BLK)
    feat_blocks = recv_feat.reshape(nblocks, BLK, FEAT)
    within = jnp.arange(tile_pixels, dtype=jnp.int32)
    block_range = jnp.arange(nblocks, dtype=jnp.int32)
    slot_range = jnp.arange(LIST, dtype=jnp.int32)

    def tile_step(totals, tile_index):
        decoder_sum, geo_acc, feat_acc = totals
        block_ids = lists[tile_index]
        count = lengths[tile_index]
        alive_mask = jnp.broadcast_to(
            (slot_range < count).astype(jnp.float32)[:, None], (LIST, BLK)
        ).reshape(LIST * BLK)
        tile_geo = jnp.take(geo_blocks, block_ids, axis=1).reshape(9, LIST * BLK)
        feat_tile = jnp.take(feat_blocks, block_ids, axis=0).reshape(LIST * BLK, FEAT)
        column = 2 * TS * (shard_index % 30) + TS * (tile_index % 2) + within % TS
        row_index = 2 * TS * (shard_index // 30) + TS * (tile_index // 2) + within // TS
        pixel_x = column.astype(jnp.float32) + 0.5
        pixel_y = row_index.astype(jnp.float32) + 0.5
        (weights, pixel_color), pullback = jax.vjp(
            lambda geo_part: composite(geo_part, alive_mask, pixel_x, pixel_y), tile_geo
        )
        weight_b = weights.astype(jnp.bfloat16)
        rendered = jnp.dot(weight_b, feat_tile, preferred_element_type=jnp.float32).astype(
            jnp.bfloat16
        )
        pred = jnp.dot(rendered, decoder, preferred_element_type=jnp.float32)
        teacher_rows = lax.dynamic_slice_in_dim(
            teacher_dev, tile_index * tile_pixels, tile_pixels, 0
        )
        error_feat = pred - teacher_rows.astype(jnp.float32)
        gpred = (error_feat / jnp.sqrt(error_feat * error_feat + 0.04)).astype(jnp.bfloat16)
        grender = lax.dot_general(
            gpred, decoder, (((1,), (1,)), ((), ())), preferred_element_type=jnp.float32
        ).astype(jnp.bfloat16)
        decoder_sum = decoder_sum + lax.dot_general(
            rendered, gpred, (((0,), (0,)), ((), ())), preferred_element_type=jnp.float32
        )
        image_cols = lax.dynamic_slice_in_dim(images_dev, tile_index * tile_pixels, tile_pixels, 1)
        error_color = pixel_color - image_cols
        gcolor = error_color / jnp.sqrt(error_color * error_color + 0.04)
        gweight = lax.dot_general(
            grender, feat_tile, (((1,), (1,)), ((), ())), preferred_element_type=jnp.float32
        )
        gfeat_tile = lax.dot_general(
            weight_b, grender, (((0,), (0,)), ((), ())), preferred_element_type=jnp.float32
        )
        (ggeo_tile,) = pullback((gweight, gcolor))
        hits = (block_ids[:, None] == block_range[None, :]).astype(jnp.float32)
        geo_acc = geo_acc + jnp.einsum(
            "clb,ln->cnb", ggeo_tile.reshape(9, LIST, BLK), hits, precision=lax.Precision.HIGHEST
        )
        feat_acc = feat_acc + jnp.einsum(
            "ln,lbf->nbf",
            hits,
            gfeat_tile.reshape(LIST, BLK, FEAT),
            precision=lax.Precision.HIGHEST,
        )
        return ((decoder_sum, geo_acc, feat_acc), None)

    start_totals = (
        jnp.zeros((FEAT, CT), jnp.float32),
        jnp.zeros((9, nblocks, BLK), jnp.float32),
        jnp.zeros((nblocks, BLK, FEAT), jnp.float32),
    )
    tile_range = jnp.arange(lists.shape[0], dtype=jnp.int32)
    (decoder_sum, geo_acc, feat_acc), _ = lax.scan(tile_step, start_totals, tile_range)
    return (decoder_sum, geo_acc.reshape(9, nblocks * BLK), feat_acc.reshape(nblocks * BLK, FEAT))


def on_device(features, geometry, decoder, teacher, images, send_index, tile_lists, tile_lengths):
    send_order = send_index[0, 0]
    shard_index = lax.axis_index("gs")
    geo_send = jnp.take(geometry[0], send_order, axis=1)
    recv_geo = lax.all_to_all(geo_send, "gs", split_axis=1, concat_axis=1, tiled=True)
    feat_send = jnp.take(features, send_order, axis=0)
    recv_feat = lax.all_to_all(feat_send, "gs", split_axis=0, concat_axis=0, tiled=True)
    decoder_sum, geo_acc, feat_acc = device_terms(
        recv_geo,
        recv_feat,
        decoder,
        teacher[0],
        images[0],
        tile_lists[0],
        tile_lengths[0],
        shard_index,
    )
    returned_geo = lax.all_to_all(geo_acc, "gs", split_axis=1, concat_axis=1, tiled=True)
    returned_feat = lax.all_to_all(feat_acc, "gs", split_axis=0, concat_axis=0, tiled=True)
    geo_own = jnp.zeros_like(returned_geo).at[:, send_order].set(returned_geo)
    feat_own = jnp.zeros_like(returned_feat).at[send_order].set(returned_feat)
    quarter = feat_own.shape[0] // lax.axis_size("view")
    summed = lax.psum(feat_own, "view")
    feature_grad = lax.dynamic_slice_in_dim(summed, lax.axis_index("view") * quarter, quarter, 0)
    pixel_total = lax.axis_size("gs") * lax.axis_size("view") * tile_lists.shape[1] * TS * TS
    decoder_grad = lax.psum(decoder_sum, ("gs", "view")) * (1.0 / math.sqrt(pixel_total))
    return (feature_grad, geo_own[None], decoder_grad)


def solution(mesh):
    placed = (
        P("gs", None),
        P("view", None, "gs"),
        P(),
        P("view", "gs", None),
        P("view", None, "gs"),
        P("view", "gs", None),
        P("view", "gs", None),
        P("view", "gs"),
    )
    return jax.shard_map(
        on_device,
        mesh=mesh,
        in_specs=placed,
        out_specs=(P(("gs", "view"), None), P("view", None, "gs"), P()),
        check_vma=False,
    )
```

profile of v0, /device:TPU:8, one launch (start us, length us, event | category | flops | bytes accessed | tf_op | source)
XLA Modules:
  0.0 610.4 jit_solution(10011325874883574381)
XLA Ops:
  10.2 2.8 gather_fusion.2
  14.1 17.4 %all-to-all-start = ((f32[9,128,8]{0,2,1:T(8,128)}), f32[9,128,8]{0,2,1:T(8,128)S(1)}, u32[]{:S(2)}, u32[]{:S(2)}) async-start(f32[9,128,8]{0,2,1:T(8,128)} %bitcast_select_fusion.1), calls=%async_computation | async-start | bytes 1048576 | tf_op jit(solution)/shard_map/all_to_all | solution.py:118
  31.5 3.2 gather_fusion.3
  35.6 16.2 %all-to-all-done = f32[9,128,8]{0,2,1:T(8,128)S(1)} async-done(((f32[9,128,8]{0,2,1:T(8,128)}), f32[9,128,8]{0,2,1:T(8,128)S(1)}, u32[]{:S(2)}, u32[]{:S(2)}) %all-to-all-start) | async-done | bytes 36896 | tf_op jit(solution)/shard_map/all_to_all | solution.py:118
  51.8 6.5 %all-to-all-start.1 = ((bf16[128,8,128]{2,1,0:T(8,128)(2,1)}), bf16[128,8,128]{2,1,0:T(8,128)(2,1)S(1)}, u32[]{:S(2)}, u32[]{:S(2)}) async-start(bf16[128,8,128]{2,1,0:T(8,128)(2,1)} %bitcast_select_fusion.2), calls=%async_computation.1 | async-start | bytes 524288 | tf_op jit(solution)/shard_map/all_to_all | solution.py:120
  60.4 12.6 %all-to-all-done.1 = bf16[128,8,128]{2,1,0:T(8,128)(2,1)S(1)} async-done(((bf16[128,8,128]{2,1,0:T(8,128)(2,1)}), bf16[128,8,128]{2,1,0:T(8,128)(2,1)S(1)}, u32[]{:S(2)}, u32[]{:S(2)}) %all-to-all-start.1) | async-done | bytes 262176 | tf_op jit(solution)/shard_map/all_to_all | solution.py:120
  73.7 187.1 %while.21 = (s32[]{:T(128)}, f32[128,512]{1,0:T(8,128)}, f32[9,8,128]{2,1,0:T(8,128)}, f32[8,128,128]{2,0,1:T(8,128)}, s32[4]{0:T(128)S(1)}, /*index=5*/s32[4]{0...) while((s32[]{:T(128)}, f32[128,512]{1,0:T(8,128)}, ...), condition=%wide.region_13.14_spmd.clone.clone, body=%wide.region_0.13_spmd.clone.clone.sunk | while | flops 448201472 | bytes 62394652 | solution.py:110
  89.3 2.2 exponential_multiply_fusion.2
  107.0 3.4 fusion.167
  114.7 2.3 fusion.168
  135.2 2.2 exponential_multiply_fusion.2
  147.6 2.3 convolution_add_fusion.8
  154.0 3.4 fusion.167
  161.7 2.3 fusion.168
  182.3 2.2 exponential_multiply_fusion.2
  194.7 2.3 convolution_add_fusion.8
  201.1 3.4 fusion.167
  208.8 2.3 fusion.168
  229.3 2.2 exponential_multiply_fusion.2
  237.1 1.8 fusion.171
  241.7 2.3 convolution_add_fusion.8
  248.1 3.4 fusion.167
  255.8 2.3 fusion.168
  260.8 1.9 copy.80
  262.7 6.5 %all-to-all-start.2 = ((f32[128,8,128]{2,1,0:T(8,128)}), f32[128,8,128]{2,1,0:T(8,128)S(1)}, u32[]{:S(2)}, u32[]{:S(2)}) async-start(f32[128,8,128]{2,1,0:T(8,128)} %bitcast.11), calls=%async_computation.2 | async-start | bytes 1048576 | tf_op jit(solution)/shard_map/all_to_all | solution.py:132
  270.0 19.5 %all-to-all-done.2 = f32[128,8,128]{2,1,0:T(8,128)S(1)} async-done(((f32[128,8,128]{2,1,0:T(8,128)}), f32[128,8,128]{2,1,0:T(8,128)S(1)}, u32[]{:S(2)}, u32[]{:S(2)}) %all-to-all-start.2) | async-done | bytes 524320 | tf_op jit(solution)/shard_map/all_to_all | solution.py:132
  289.5 4.0 scatter_custom_fusion
  295.4 6.4 %all-to-all-start.3 = ((f32[9,128,8]{0,2,1:T(8,128)}), f32[9,128,8]{0,2,1:T(8,128)S(1)}, u32[]{:S(2)}, u32[]{:S(2)}) async-start(f32[9,128,8]{0,2,1:T(8,128)} %bitcast.13), calls=%async_computation.3 | async-start | bytes 1048576 | tf_op jit(solution)/shard_map/all_to_all | solution.py:131
  301.7 20.4 %all-to-all-done.3 = f32[9,128,8]{0,2,1:T(8,128)S(1)} async-done(((f32[9,128,8]{0,2,1:T(8,128)}), f32[9,128,8]{0,2,1:T(8,128)S(1)}, u32[]{:S(2)}, u32[]{:S(2)}) %all-to-all-start.3) | async-done | bytes 36896 | tf_op jit(solution)/shard_map/all_to_all | solution.py:131
  322.2 3.4 scatter_custom_fusion.1
  326.4 222.5 %all-reduce.14.cloned.1.call-done = f32[128,512]{1,0:T(8,128)} async-done(((f32[128,512]{1,0:T(8,128)}), f32[128,512]{1,0:T(8,128)}) %all-reduce.14.cloned.1.call-update) | async-done | bytes 262160 | tf_op jit(solution)/shard_map/psum | solution.py:139
  550.5 51.4 %all-reduce.12.cloned.1.call-done = f32[1024,128]{1,0:T(8,128)} async-done(((f32[1024,128]{1,0:T(8,128)}), f32[1024,128]{1,0:T(8,128)}) %all-reduce.12.cloned.1.call-update) | async-done | bytes 524304 | tf_op jit(solution)/shard_map/psum | solution.py:136
  (517 shorter events, 140.9 us)
Async XLA Ops:
  7.2 24.3 %copy-start = (bf16[1024,128]{1,0:T(8,128)(2,1)S(1)}, bf16[1024,128]{1,0:T(8,128)(2,1)}, u32[]{:S(2)}) copy-start(bf16[1024,128]{1,0:T(8,128)(2,1)} %param.10) | copy-start | bytes 786436
  14.1 37.7 %all-to-all-start = ((f32[9,128,8]{0,2,1:T(8,128)}), f32[9,128,8]{0,2,1:T(8,128)S(1)}, u32[]{:S(2)}, u32[]{:S(2)}) async-start(f32[9,128,8]{0,2,1:T(8,128)} %bitcast_select_fusion.1), calls=%async_computation | async-start | bytes 1048576 | tf_op jit(solution)/shard_map/all_to_all | solution.py:118
  51.8 21.3 %all-to-all-start.1 = ((bf16[128,8,128]{2,1,0:T(8,128)(2,1)}), bf16[128,8,128]{2,1,0:T(8,128)(2,1)S(1)}, u32[]{:S(2)}, u32[]{:S(2)}) async-start(bf16[128,8,128]{2,1,0:T(8,128)(2,1)} %bitcast_select_fusion.2), calls=%async_computation.1 | async-start | bytes 524288 | tf_op jit(solution)/shard_map/all_to_all | solution.py:120
  73.7 13.7 %copy-start.8 = (bf16[8,128,128]{2,1,0:T(8,128)(2,1)}, bf16[8,128,128]{2,1,0:T(8,128)(2,1)S(1)}, u32[]{:S(2)}) copy-start(bf16[8,128,128]{2,1,0:T(8,128)(2,1)S(1)} %get-tuple-element.843) | copy-start | bytes 786436 | tf_op jit(solution)/shard_map/while
  81.3 22.9 %copy-start.21 = (f32[256]{0:T(256)}, f32[256]{0:T(256)S(1)}, u32[]{:S(2)}) copy-start(f32[256]{0:T(256)S(1)} %get-tuple-element.768) | copy-start | bytes 3076 | tf_op jit(solution)/shard_map/while
  81.3 22.9 %copy-start.23 = (f32[256]{0:T(256)}, f32[256]{0:T(256)S(1)}, u32[]{:S(2)}) copy-start(f32[256]{0:T(256)S(1)} %get-tuple-element.765) | copy-start | bytes 3076 | tf_op jit(solution)/shard_map/while
  82.0 19.6 %copy-start.28 = (s32[8]{0:T(128)}, s32[8]{0:T(128)S(1)}, u32[]{:S(2)}) copy-start(s32[8]{0:T(128)S(1)} %get-tuple-element.785) | copy-start | bytes 100 | tf_op jit(solution)/shard_map/while
  84.2 18.9 %copy-start.5 = (f32[9,8,128]{2,0,1:T(8,128)}, f32[9,8,128]{2,0,1:T(8,128)S(1)}, u32[]{:S(2)}) copy-start(f32[9,8,128]{2,0,1:T(8,128)S(1)} %select_bitcast_fusion.2) | copy-start | bytes 110596 | tf_op jit(solution)/shard_map/while
  84.9 19.4 %copy-start.11 = (f32[1,8,128]{2,0,1:T(1,128)}, f32[1,8,128]{2,0,1:T(1,128)S(1)}, u32[]{:S(2)}) copy-start(f32[1,8,128]{2,0,1:T(1,128)S(1)} %get-tuple-element.769) | copy-start | bytes 12292 | tf_op jit(solution)/shard_map/while
  85.5 18.8 %copy-start.16 = (f32[1024]{0:T(1024)}, f32[1024]{0:T(1024)S(1)}, u32[]{:S(2)}) copy-start(f32[1024]{0:T(1024)S(1)} %bitcast_multiply_fusion.8) | copy-start | bytes 12292 | tf_op jit(solution)/shard_map/while
  127.3 24.0 %copy-start.21 = (f32[256]{0:T(256)}, f32[256]{0:T(256)S(1)}, u32[]{:S(2)}) copy-start(f32[256]{0:T(256)S(1)} %get-tuple-element.768) | copy-start | bytes 3076 | tf_op jit(solution)/shard_map/while
  127.3 24.0 %copy-start.23 = (f32[256]{0:T(256)}, f32[256]{0:T(256)S(1)}, u32[]{:S(2)}) copy-start(f32[256]{0:T(256)S(1)} %get-tuple-element.765) | copy-start | bytes 3076 | tf_op jit(solution)/shard_map/while
  128.0 19.6 %copy-start.28 = (s32[8]{0:T(128)}, s32[8]{0:T(128)S(1)}, u32[]{:S(2)}) copy-start(s32[8]{0:T(128)S(1)} %get-tuple-element.785) | copy-start | bytes 100 | tf_op jit(solution)/shard_map/while
  130.2 20.0 %copy-start.5 = (f32[9,8,128]{2,0,1:T(8,128)}, f32[9,8,128]{2,0,1:T(8,128)S(1)}, u32[]{:S(2)}) copy-start(f32[9,8,128]{2,0,1:T(8,128)S(1)} %select_bitcast_fusion.2) | copy-start | bytes 110596 | tf_op jit(solution)/shard_map/while
  130.8 20.5 %copy-start.11 = (f32[1,8,128]{2,0,1:T(1,128)}, f32[1,8,128]{2,0,1:T(1,128)S(1)}, u32[]{:S(2)}) copy-start(f32[1,8,128]{2,0,1:T(1,128)S(1)} %get-tuple-element.769) | copy-start | bytes 12292 | tf_op jit(solution)/shard_map/while
  131.4 19.9 %copy-start.16 = (f32[1024]{0:T(1024)}, f32[1024]{0:T(1024)S(1)}, u32[]{:S(2)}) copy-start(f32[1024]{0:T(1024)S(1)} %bitcast_multiply_fusion.8) | copy-start | bytes 12292 | tf_op jit(solution)/shard_map/while
  174.3 24.0 %copy-start.21 = (f32[256]{0:T(256)}, f32[256]{0:T(256)S(1)}, u32[]{:S(2)}) copy-start(f32[256]{0:T(256)S(1)} %get-tuple-element.768) | copy-start | bytes 3076 | tf_op jit(solution)/shard_map/while
  174.3 24.0 %copy-start.23 = (f32[256]{0:T(256)}, f32[256]{0:T(256)S(1)}, u32[]{:S(2)}) copy-start(f32[256]{0:T(256)S(1)} %get-tuple-element.765) | copy-start | bytes 3076 | tf_op jit(solution)/shard_map/while
  175.0 19.6 %copy-start.28 = (s32[8]{0:T(128)}, s32[8]{0:T(128)S(1)}, u32[]{:S(2)}) copy-start(s32[8]{0:T(128)S(1)} %get-tuple-element.785) | copy-start | bytes 100 | tf_op jit(solution)/shard_map/while
  177.2 20.0 %copy-start.5 = (f32[9,8,128]{2,0,1:T(8,128)}, f32[9,8,128]{2,0,1:T(8,128)S(1)}, u32[]{:S(2)}) copy-start(f32[9,8,128]{2,0,1:T(8,128)S(1)} %select_bitcast_fusion.2) | copy-start | bytes 110596 | tf_op jit(solution)/shard_map/while
  177.8 20.5 %copy-start.11 = (f32[1,8,128]{2,0,1:T(1,128)}, f32[1,8,128]{2,0,1:T(1,128)S(1)}, u32[]{:S(2)}) copy-start(f32[1,8,128]{2,0,1:T(1,128)S(1)} %get-tuple-element.769) | copy-start | bytes 12292 | tf_op jit(solution)/shard_map/while
  178.4 19.9 %copy-start.16 = (f32[1024]{0:T(1024)}, f32[1024]{0:T(1024)S(1)}, u32[]{:S(2)}) copy-start(f32[1024]{0:T(1024)S(1)} %bitcast_multiply_fusion.8) | copy-start | bytes 12292 | tf_op jit(solution)/shard_map/while
  221.3 24.0 %copy-start.21 = (f32[256]{0:T(256)}, f32[256]{0:T(256)S(1)}, u32[]{:S(2)}) copy-start(f32[256]{0:T(256)S(1)} %get-tuple-element.768) | copy-start | bytes 3076 | tf_op jit(solution)/shard_map/while
  221.3 24.0 %copy-start.23 = (f32[256]{0:T(256)}, f32[256]{0:T(256)S(1)}, u32[]{:S(2)}) copy-start(f32[256]{0:T(256)S(1)} %get-tuple-element.765) | copy-start | bytes 3076 | tf_op jit(solution)/shard_map/while
  222.0 19.6 %copy-start.28 = (s32[8]{0:T(128)}, s32[8]{0:T(128)S(1)}, u32[]{:S(2)}) copy-start(s32[8]{0:T(128)S(1)} %get-tuple-element.785) | copy-start | bytes 100 | tf_op jit(solution)/shard_map/while
  224.2 20.0 %copy-start.5 = (f32[9,8,128]{2,0,1:T(8,128)}, f32[9,8,128]{2,0,1:T(8,128)S(1)}, u32[]{:S(2)}) copy-start(f32[9,8,128]{2,0,1:T(8,128)S(1)} %select_bitcast_fusion.2) | copy-start | bytes 110596 | tf_op jit(solution)/shard_map/while
  224.9 20.5 %copy-start.11 = (f32[1,8,128]{2,0,1:T(1,128)}, f32[1,8,128]{2,0,1:T(1,128)S(1)}, u32[]{:S(2)}) copy-start(f32[1,8,128]{2,0,1:T(1,128)S(1)} %get-tuple-element.769) | copy-start | bytes 12292 | tf_op jit(solution)/shard_map/while
  225.5 19.9 %copy-start.16 = (f32[1024]{0:T(1024)}, f32[1024]{0:T(1024)S(1)}, u32[]{:S(2)}) copy-start(f32[1024]{0:T(1024)S(1)} %bitcast_multiply_fusion.8) | copy-start | bytes 12292 | tf_op jit(solution)/shard_map/while
  262.7 26.8 %all-to-all-start.2 = ((f32[128,8,128]{2,1,0:T(8,128)}), f32[128,8,128]{2,1,0:T(8,128)S(1)}, u32[]{:S(2)}, u32[]{:S(2)}) async-start(f32[128,8,128]{2,1,0:T(8,128)} %bitcast.11), calls=%async_computation.2 | async-start | bytes 1048576 | tf_op jit(solution)/shard_map/all_to_all | solution.py:132
  269.2 279.6 %all-reduce.14.cloned.1.call-start = ((), (), s32[]{:S(2)}) async-start(), calls=%async_computation.5 | async-start | bytes 524288 | tf_op jit(solution)/shard_map/psum | solution.py:139
  269.9 332.0 %all-reduce.12.cloned.1.call-start = ((), (), s32[]{:S(2)}) async-start(), calls=%async_computation.4 | async-start | bytes 1048576 | tf_op jit(solution)/shard_map/psum | solution.py:136
  295.4 26.8 %all-to-all-start.3 = ((f32[9,128,8]{0,2,1:T(8,128)}), f32[9,128,8]{0,2,1:T(8,128)S(1)}, u32[]{:S(2)}, u32[]{:S(2)}) async-start(f32[9,128,8]{0,2,1:T(8,128)} %bitcast.13), calls=%async_computation.3 | async-start | bytes 1048576 | tf_op jit(solution)/shard_map/all_to_all | solution.py:131
  (105 other events, 181.8 us)
Sparse Core Ops, SparseCore 0:
  275.6 273.1 all-reduce.13
  551.3 50.6 all-reduce.11
where the time goes:
time: 613 us; the launch traced here: 610 us
  waiting for transfers between devices  343 us (56%)
  local copies, waits for them, and re-layouts  79.9 us (13%)
  other arithmetic  76.6 us (12%)
  matrix products  39.1 us (6%)
  starting transfers between devices  36.8 us (6%)
  loops' own time  20.3 us (3%)
  between operations  14.3 us (2%)
    psum x1, waiting for transfers between devices, on_device(): lax.psum(decoder_sum, ('gs', 'view')) * (1.0 / math.sqrt(pixel_total))  222 us
    psum x1, waiting for transfers between devices, on_device(): summed = lax.psum(feat_own, 'view')  51.4 us
    another operation x8, other arithmetic, composite(): inner = jnp.cumsum(blocked, axis=2) - blocked  22.4 us
    all_to_all x1, waiting for transfers between devices, on_device(): lax.all_to_all(geo_acc, 'gs', split_axis=1, concat_axis=1, tiled=True)  20.4 us
    another operation x1, loops' own time, device_terms(): lax.scan(tile_step, start_totals, tile_range)  20.3 us
    all_to_all x1, waiting for transfers between devices, on_device(): lax.all_to_all(feat_acc, 'gs', split_axis=0, concat_axis=0, tiled=True)  19.5 us
    while x264, local copies, waits for them, and re-layouts  19.3 us
    all_to_all x1, starting transfers between devices, on_device(): lax.all_to_all(geo_send, 'gs', split_axis=1, concat_axis=1, tiled=True)  17.4 us
  transfers between devices with their start and end apart: 6, of which 6 were waited for; matrix products, arithmetic and copies ran while one was open for 3% of the time, Pallas kernels for 0%

commit v1 on v0

--- a/solution.py
+++ b/solution.py
@@ -128,7 +128,10 @@
         tile_lengths[0],
         shard_index,
     )
-    returned_geo = lax.all_to_all(geo_acc, "gs", split_axis=1, concat_axis=1, tiled=True)
+    returned_geo = jnp.concatenate(
+        lax.all_to_all(jnp.stack(jnp.split(geo_acc, lax.axis_size("gs"), axis=1)), "gs", 0, 0),
+        axis=1,
+    )
     returned_feat = lax.all_to_all(feat_acc, "gs", split_axis=0, concat_axis=0, tiled=True)
     geo_own = jnp.zeros_like(returned_geo).at[:, send_order].set(returned_geo)
     feat_own = jnp.zeros_like(returned_feat).at[send_order].set(returned_feat)

time: 613 us -> 589 us (0.961)
  waiting for transfers between devices: 343 us -> 241 us
  local copies, waits for them, and re-layouts: 79.9 us -> 150 us
  starting transfers between devices: 36.8 us -> 44.2 us
    psum x1, waiting for transfers between devices: 222 us -> 140 us  [on_device(): lax.psum(decoder_sum, ('gs', 'view')) * (1.0 / math.sqrt(pixel_total))]
    unnamed x19 -> x146, local copies, waits for them, and re-layouts: 5.75 us -> 79.4 us
    all_to_all x1, waiting for transfers between devices: 19.5 us -> 0.01 us  [on_device(): lax.all_to_all(feat_acc, 'gs', split_axis=0, concat_axis=0, tiled=True)]
    all_to_all x1, starting transfers between devices: 6.36 us -> 13.7 us  [on_device(): lax.all_to_all(jnp.stack(jnp.split(geo_acc, lax.axis_size('gs'), axis=1))...]
    while x264 -> x280, local copies, waits for them, and re-layouts: 19.3 us -> 19.2 us
  transfers between devices with their start and end apart: 6 -> 6, of which waited for: 6 -> 5; matrix products, arithmetic and copies ran while one was open for 3% -> 15% of each run, Pallas kernels for 0% -> 0%
where the time goes in v1:
time: 589 us; the launch traced here: 586 us
  waiting for transfers between devices  241 us (41%)
  local copies, waits for them, and re-layouts  150 us (25%)
  other arithmetic  76.6 us (13%)
  starting transfers between devices  44.2 us (8%)
  matrix products  39.2 us (7%)
  loops' own time  20.6 us (3%)
  between operations  14.4 us (2%)
    psum x1, waiting for transfers between devices, on_device(): lax.psum(decoder_sum, ('gs', 'view')) * (1.0 / math.sqrt(pixel_total))  140 us
    unnamed x146, local copies, waits for them, and re-layouts  79.4 us
    psum x1, waiting for transfers between devices, on_device(): summed = lax.psum(feat_own, 'view')  51.4 us
    another operation x8, other arithmetic, composite(): inner = jnp.cumsum(blocked, axis=2) - blocked  22.4 us
    another operation x1, loops' own time, device_terms(): lax.scan(tile_step, start_totals, tile_range)  20.6 us
    all_to_all x1, waiting for transfers between devices, on_device(): lax.all_to_all(jnp.stack(jnp.split(geo_acc, lax.axis_size('gs'), axis=1))...  20.4 us
    while x280, local copies, waits for them, and re-layouts  19.2 us
    all_to_all x1, starting transfers between devices, on_device(): lax.all_to_all(geo_send, 'gs', split_axis=1, concat_axis=1, tiled=True)  17.4 us
  transfers between devices with their start and end apart: 6, of which 5 were waited for; matrix products, arithmetic and copies ran while one was open for 15% of the time, Pallas kernels for 0%

profile of v1, /device:TPU:8, one launch (start us, length us, event | category | flops | bytes accessed | tf_op | source)
XLA Modules:
  0.0 586.3 jit_solution(11409221392307989041)
XLA Ops:
  10.2 2.8 gather_fusion.2
  14.1 17.4 %all-to-all-start = ((f32[9,128,8]{0,2,1:T(8,128)}), f32[9,128,8]{0,2,1:T(8,128)S(1)}, u32[]{:S(2)}, u32[]{:S(2)}) async-start(f32[9,128,8]{0,2,1:T(8,128)} %bitcast_select_fusion.1), calls=%async_computation | async-start | bytes 1048576 | tf_op jit(solution)/shard_map/all_to_all | solution.py:118
  31.4 3.2 gather_fusion.3
  35.6 16.2 %all-to-all-done = f32[9,128,8]{0,2,1:T(8,128)S(1)} async-done(((f32[9,128,8]{0,2,1:T(8,128)}), f32[9,128,8]{0,2,1:T(8,128)S(1)}, u32[]{:S(2)}, u32[]{:S(2)}) %all-to-all-start) | async-done | bytes 36896 | tf_op jit(solution)/shard_map/all_to_all | solution.py:118
  51.7 6.5 %all-to-all-start.1 = ((bf16[128,8,128]{2,1,0:T(8,128)(2,1)}), bf16[128,8,128]{2,1,0:T(8,128)(2,1)S(1)}, u32[]{:S(2)}, u32[]{:S(2)}) async-start(bf16[128,8,128]{2,1,0:T(8,128)(2,1)} %bitcast_select_fusion.2), calls=%async_computation.1 | async-start | bytes 524288 | tf_op jit(solution)/shard_map/all_to_all | solution.py:120
  59.8 13.2 %all-to-all-done.1 = bf16[128,8,128]{2,1,0:T(8,128)(2,1)S(1)} async-done(((bf16[128,8,128]{2,1,0:T(8,128)(2,1)}), bf16[128,8,128]{2,1,0:T(8,128)(2,1)S(1)}, u32[]{:S(2)}, u32[]{:S(2)}) %all-to-all-start.1) | async-done | bytes 262176 | tf_op jit(solution)/shard_map/all_to_all | solution.py:120
  73.6 184.3 %while.21 = (s32[]{:T(128)}, f32[128,512]{1,0:T(8,128)}, f32[9,8,128]{2,1,0:T(8,128)}, f32[8,128,128]{2,0,1:T(8,128)}, s32[4]{0:T(128)S(1)}, /*index=5*/s32[4]{0...) while((s32[]{:T(128)}, f32[128,512]{1,0:T(8,128)}, ...), condition=%wide.region_13.14_spmd.clone.clone, body=%wide.region_0.13_spmd.clone.clone.sunk | while | flops 448201472 | bytes 62689620 | solution.py:110
  88.5 2.2 exponential_multiply_fusion.2
  96.3 1.8 fusion.171
  106.3 3.4 fusion.167
  113.9 2.3 fusion.168
  133.7 2.2 exponential_multiply_fusion.2
  146.1 2.3 convolution_add_fusion.8
  152.6 3.4 fusion.167
  160.2 2.3 fusion.168
  180.0 2.2 exponential_multiply_fusion.2
  187.8 1.8 fusion.171
  192.4 2.3 convolution_add_fusion.8
  198.9 3.4 fusion.167
  206.5 2.3 fusion.168
  226.3 2.2 exponential_multiply_fusion.2
  238.7 2.3 convolution_add_fusion.8
  245.1 3.4 fusion.167
  252.8 2.3 fusion.168
  257.9 1.9 copy.657
  259.9 6.5 %all-to-all-start.2 = ((f32[128,8,128]{2,1,0:T(8,128)}), f32[128,8,128]{2,1,0:T(8,128)S(1)}, u32[]{:S(2)}, u32[]{:S(2)}) async-start(f32[128,8,128]{2,1,0:T(8,128)} %bitcast.11), calls=%async_computation.2 | async-start | bytes 1048576 | tf_op jit(solution)/shard_map/all_to_all | solution.py:135
  341.8 4.0 scatter_custom_fusion
  346.4 13.7 %all-to-all-start.3 = ((f32[128,9,8]{1,2,0:T(8,128)}), f32[128,9,8]{1,2,0:T(8,128)S(1)}, u32[]{:S(2)}, u32[]{:S(2)}) async-start(f32[128,9,8]{1,2,0:T(8,128)} %constant_dynamic-update-slice_fusion), calls=%async_computation.3 | async-start | bytes 1048576 | tf_op jit(solution)/shard_map/all_to_all | solution.py:132
  360.2 20.4 %all-to-all-done.3 = f32[128,9,8]{1,2,0:T(8,128)S(1)} async-done(((f32[128,9,8]{1,2,0:T(8,128)}), f32[128,9,8]{1,2,0:T(8,128)S(1)}, u32[]{:S(2)}, u32[]{:S(2)}) %all-to-all-start.3) | async-done | bytes 36896 | tf_op jit(solution)/shard_map/all_to_all | solution.py:132
  380.5 3.4 scatter_custom_fusion.1
  384.7 140.1 %all-reduce.14.cloned.1.call-done = f32[128,512]{1,0:T(8,128)} async-done(((f32[128,512]{1,0:T(8,128)}), f32[128,512]{1,0:T(8,128)}) %all-reduce.14.cloned.1.call-update) | async-done | bytes 262160 | tf_op jit(solution)/shard_map/psum | solution.py:142
  526.5 51.4 %all-reduce.12.cloned.1.call-done = f32[1024,128]{1,0:T(8,128)} async-done(((f32[1024,128]{1,0:T(8,128)}), f32[1024,128]{1,0:T(8,128)}) %all-reduce.12.cloned.1.call-update) | async-done | bytes 524304 | tf_op jit(solution)/shard_map/psum | solution.py:139
  (661 shorter events, 208.6 us)
Async XLA Ops:
  7.2 24.3 %copy-start = (bf16[1024,128]{1,0:T(8,128)(2,1)S(1)}, bf16[1024,128]{1,0:T(8,128)(2,1)}, u32[]{:S(2)}) copy-start(bf16[1024,128]{1,0:T(8,128)(2,1)} %param.10) | copy-start | bytes 786436
  14.1 37.7 %all-to-all-start = ((f32[9,128,8]{0,2,1:T(8,128)}), f32[9,128,8]{0,2,1:T(8,128)S(1)}, u32[]{:S(2)}, u32[]{:S(2)}) async-start(f32[9,128,8]{0,2,1:T(8,128)} %bitcast_select_fusion.1), calls=%async_computation | async-start | bytes 1048576 | tf_op jit(solution)/shard_map/all_to_all | solution.py:118
  51.7 21.2 %all-to-all-start.1 = ((bf16[128,8,128]{2,1,0:T(8,128)(2,1)}), bf16[128,8,128]{2,1,0:T(8,128)(2,1)S(1)}, u32[]{:S(2)}, u32[]{:S(2)}) async-start(bf16[128,8,128]{2,1,0:T(8,128)(2,1)} %bitcast_select_fusion.2), calls=%async_computation.1 | async-start | bytes 524288 | tf_op jit(solution)/shard_map/all_to_all | solution.py:120
  58.2 466.6 %all-reduce.14.cloned.1.call-start = ((), (), s32[]{:S(2)}) async-start(), calls=%async_computation.5 | async-start | bytes 524288 | tf_op jit(solution)/shard_map/psum | solution.py:142
  73.7 12.9 %copy-start.8 = (bf16[8,128,128]{2,1,0:T(8,128)(2,1)}, bf16[8,128,128]{2,1,0:T(8,128)(2,1)S(1)}, u32[]{:S(2)}) copy-start(bf16[8,128,128]{2,1,0:T(8,128)(2,1)S(1)} %get-tuple-element.894) | copy-start | bytes 786436 | tf_op jit(solution)/shard_map/while
  81.4 22.1 %copy-start.23 = (f32[256]{0:T(256)}, f32[256]{0:T(256)S(1)}, u32[]{:S(2)}) copy-start(f32[256]{0:T(256)S(1)} %get-tuple-element.819) | copy-start | bytes 3076 | tf_op jit(solution)/shard_map/while
  81.4 22.1 %copy-start.25 = (f32[256]{0:T(256)}, f32[256]{0:T(256)S(1)}, u32[]{:S(2)}) copy-start(f32[256]{0:T(256)S(1)} %get-tuple-element.816) | copy-start | bytes 3076 | tf_op jit(solution)/shard_map/while
  82.1 18.8 %copy-start.30 = (s32[8]{0:T(128)}, s32[8]{0:T(128)S(1)}, u32[]{:S(2)}) copy-start(s32[8]{0:T(128)S(1)} %get-tuple-element.836) | copy-start | bytes 100 | tf_op jit(solution)/shard_map/while
  83.4 19.0 %copy-start.5 = (f32[9,8,128]{2,0,1:T(8,128)}, f32[9,8,128]{2,0,1:T(8,128)S(1)}, u32[]{:S(2)}) copy-start(f32[9,8,128]{2,0,1:T(8,128)S(1)} %select_bitcast_fusion.2) | copy-start | bytes 110596 | tf_op jit(solution)/shard_map/while
  84.1 19.4 %copy-start.11 = (f32[1,8,128]{2,0,1:T(1,128)}, f32[1,8,128]{2,0,1:T(1,128)S(1)}, u32[]{:S(2)}) copy-start(f32[1,8,128]{2,0,1:T(1,128)S(1)} %get-tuple-element.820) | copy-start | bytes 12292 | tf_op jit(solution)/shard_map/while
  84.7 18.9 %copy-start.16 = (f32[1024]{0:T(1024)}, f32[1024]{0:T(1024)S(1)}, u32[]{:S(2)}) copy-start(f32[1024]{0:T(1024)S(1)} %bitcast_multiply_fusion.8) | copy-start | bytes 12292 | tf_op jit(solution)/shard_map/while
  126.5 23.2 %copy-start.23 = (f32[256]{0:T(256)}, f32[256]{0:T(256)S(1)}, u32[]{:S(2)}) copy-start(f32[256]{0:T(256)S(1)} %get-tuple-element.819) | copy-start | bytes 3076 | tf_op jit(solution)/shard_map/while
  126.6 23.2 %copy-start.25 = (f32[256]{0:T(256)}, f32[256]{0:T(256)S(1)}, u32[]{:S(2)}) copy-start(f32[256]{0:T(256)S(1)} %get-tuple-element.816) | copy-start | bytes 3076 | tf_op jit(solution)/shard_map/while
  127.3 18.8 %copy-start.30 = (s32[8]{0:T(128)}, s32[8]{0:T(128)S(1)}, u32[]{:S(2)}) copy-start(s32[8]{0:T(128)S(1)} %get-tuple-element.836) | copy-start | bytes 100 | tf_op jit(solution)/shard_map/while
  128.6 20.1 %copy-start.5 = (f32[9,8,128]{2,0,1:T(8,128)}, f32[9,8,128]{2,0,1:T(8,128)S(1)}, u32[]{:S(2)}) copy-start(f32[9,8,128]{2,0,1:T(8,128)S(1)} %select_bitcast_fusion.2) | copy-start | bytes 110596 | tf_op jit(solution)/shard_map/while
  129.3 20.5 %copy-start.11 = (f32[1,8,128]{2,0,1:T(1,128)}, f32[1,8,128]{2,0,1:T(1,128)S(1)}, u32[]{:S(2)}) copy-start(f32[1,8,128]{2,0,1:T(1,128)S(1)} %get-tuple-element.820) | copy-start | bytes 12292 | tf_op jit(solution)/shard_map/while
  129.9 20.0 %copy-start.16 = (f32[1024]{0:T(1024)}, f32[1024]{0:T(1024)S(1)}, u32[]{:S(2)}) copy-start(f32[1024]{0:T(1024)S(1)} %bitcast_multiply_fusion.8) | copy-start | bytes 12292 | tf_op jit(solution)/shard_map/while
  172.8 23.2 %copy-start.23 = (f32[256]{0:T(256)}, f32[256]{0:T(256)S(1)}, u32[]{:S(2)}) copy-start(f32[256]{0:T(256)S(1)} %get-tuple-element.819) | copy-start | bytes 3076 | tf_op jit(solution)/shard_map/while
  172.8 23.2 %copy-start.25 = (f32[256]{0:T(256)}, f32[256]{0:T(256)S(1)}, u32[]{:S(2)}) copy-start(f32[256]{0:T(256)S(1)} %get-tuple-element.816) | copy-start | bytes 3076 | tf_op jit(solution)/shard_map/while
  173.5 18.8 %copy-start.30 = (s32[8]{0:T(128)}, s32[8]{0:T(128)S(1)}, u32[]{:S(2)}) copy-start(s32[8]{0:T(128)S(1)} %get-tuple-element.836) | copy-start | bytes 100 | tf_op jit(solution)/shard_map/while
  174.9 20.1 %copy-start.5 = (f32[9,8,128]{2,0,1:T(8,128)}, f32[9,8,128]{2,0,1:T(8,128)S(1)}, u32[]{:S(2)}) copy-start(f32[9,8,128]{2,0,1:T(8,128)S(1)} %select_bitcast_fusion.2) | copy-start | bytes 110596 | tf_op jit(solution)/shard_map/while
  175.6 20.5 %copy-start.11 = (f32[1,8,128]{2,0,1:T(1,128)}, f32[1,8,128]{2,0,1:T(1,128)S(1)}, u32[]{:S(2)}) copy-start(f32[1,8,128]{2,0,1:T(1,128)S(1)} %get-tuple-element.820) | copy-start | bytes 12292 | tf_op jit(solution)/shard_map/while
  176.2 20.0 %copy-start.16 = (f32[1024]{0:T(1024)}, f32[1024]{0:T(1024)S(1)}, u32[]{:S(2)}) copy-start(f32[1024]{0:T(1024)S(1)} %bitcast_multiply_fusion.8) | copy-start | bytes 12292 | tf_op jit(solution)/shard_map/while
  219.1 23.2 %copy-start.23 = (f32[256]{0:T(256)}, f32[256]{0:T(256)S(1)}, u32[]{:S(2)}) copy-start(f32[256]{0:T(256)S(1)} %get-tuple-element.819) | copy-start | bytes 3076 | tf_op jit(solution)/shard_map/while
  219.1 23.3 %copy-start.25 = (f32[256]{0:T(256)}, f32[256]{0:T(256)S(1)}, u32[]{:S(2)}) copy-start(f32[256]{0:T(256)S(1)} %get-tuple-element.816) | copy-start | bytes 3076 | tf_op jit(solution)/shard_map/while
  219.8 18.8 %copy-start.30 = (s32[8]{0:T(128)}, s32[8]{0:T(128)S(1)}, u32[]{:S(2)}) copy-start(s32[8]{0:T(128)S(1)} %get-tuple-element.836) | copy-start | bytes 100 | tf_op jit(solution)/shard_map/while
  221.2 20.1 %copy-start.5 = (f32[9,8,128]{2,0,1:T(8,128)}, f32[9,8,128]{2,0,1:T(8,128)S(1)}, u32[]{:S(2)}) copy-start(f32[9,8,128]{2,0,1:T(8,128)S(1)} %select_bitcast_fusion.2) | copy-start | bytes 110596 | tf_op jit(solution)/shard_map/while
  221.9 20.5 %copy-start.11 = (f32[1,8,128]{2,0,1:T(1,128)}, f32[1,8,128]{2,0,1:T(1,128)S(1)}, u32[]{:S(2)}) copy-start(f32[1,8,128]{2,0,1:T(1,128)S(1)} %get-tuple-element.820) | copy-start | bytes 12292 | tf_op jit(solution)/shard_map/while
  222.4 20.0 %copy-start.16 = (f32[1024]{0:T(1024)}, f32[1024]{0:T(1024)S(1)}, u32[]{:S(2)}) copy-start(f32[1024]{0:T(1024)S(1)} %bitcast_multiply_fusion.8) | copy-start | bytes 12292 | tf_op jit(solution)/shard_map/while
  259.9 81.9 %all-to-all-start.2 = ((f32[128,8,128]{2,1,0:T(8,128)}), f32[128,8,128]{2,1,0:T(8,128)S(1)}, u32[]{:S(2)}, u32[]{:S(2)}) async-start(f32[128,8,128]{2,1,0:T(8,128)} %bitcast.11), calls=%async_computation.2 | async-start | bytes 1048576 | tf_op jit(solution)/shard_map/all_to_all | solution.py:135
  266.4 311.5 %all-reduce.12.cloned.1.call-start = ((), (), s32[]{:S(2)}) async-start(), calls=%async_computation.4 | async-start | bytes 1048576 | tf_op jit(solution)/shard_map/psum | solution.py:139
  346.4 34.1 %all-to-all-start.3 = ((f32[128,9,8]{1,2,0:T(8,128)}), f32[128,9,8]{1,2,0:T(8,128)S(1)}, u32[]{:S(2)}, u32[]{:S(2)}) async-start(f32[128,9,8]{1,2,0:T(8,128)} %constant_dynamic-update-slice_fusion), calls=%async_computation.3 | async-start | bytes 1048576 | tf_op jit(solution)/shard_map/all_to_all | solution.py:132
  (113 other events, 233.4 us)
Sparse Core Ops, SparseCore 0:
  260.0 264.7 all-reduce.13
  527.2 50.6 all-reduce.11
